TPU v7x, 512 devices: a whole 4x4x16 slice. The times are simulated.
512 devices in a mesh: takers: 64 (over z, x), nodes: 8 (over y, core).
Axes of the slice: x: 4, y: 4, z: 16, core: 2. Of those that a mesh axis runs over, the one named last changes fastest.
Arguments:
- slopes: bfloat16 [3, 65536], P(None, 'takers'), may hold values from 0.29882812 to 1.5
- intercepts: bfloat16 [65536], P('takers'), may hold values from -3 to 3
- guessing: bfloat16 [65536], P('takers'), may hold values from 0.049804688 to 0.29882812
- responses: int32 [256, 12, 128, 128], P('takers'), may hold values from 0 to 2, as said below
- tile_items: int32 [256, 12], P('takers'), may hold values from 0 to 511, as said below
- tile_count: int32 [256], P('takers'), may hold values from 4 to 12, as said below
Outputs:
- new_params: float32 [4, 65536], P(None, 'takers')
- marginal: float32 [32768], P('takers')
- posterior_mean: float32 [3, 32768], P(None, 'takers')
Inputs may be any that keep to these rules, and one draw needn't show every extreme that they name: `tile_items`: within a row block the used slots name distinct item blocks; some row block uses all 12 slots. `tile_count`: some row block uses all 12 slots; slots at or beyond the count are ignored. `responses`: 0 means not answered, 1 a wrong answer, 2 a right answer; most entries are 0.
All inputs are finite; a program needn't handle non-finite values.
Results may differ from a plain program's by a relative error of at most 0.0041.
Values may be sent and summed in bfloat16 or wider, within the bound.
No kernel may reach another device: no remote copies, remote signals or barrier semaphores. Data moves between devices by JAX's collectives and lax.ppermute only.
A program may use at most 64 MiB of HBM per device.

v0:
```python
import jax
import jax.numpy as jnp
from jax import lax
from jax.sharding import PartitionSpec as P

NODES_1D = 16


def node_grid(first_node, how_many, grid_side):
    node_index = first_node + jnp.arange(how_many, dtype=jnp.int32)
    lattice = jnp.stack(
        [
            node_index // (grid_side * grid_side),
            node_index // grid_side % grid_side,
            node_index % grid_side,
        ]
    ).astype(jnp.float32)
    return -3.0 + 6.0 * lattice / (grid_side - 1)


def log_prior(node_points, grid_side):
    whole = node_grid(0, grid_side**3, grid_side)
    log_total = jnp.log(jnp.sum(jnp.exp(-0.5 * jnp.sum(whole * whole, axis=0))))
    return -0.5 * jnp.sum(node_points * node_points, axis=0) - log_total


def tile_logits(slope_blk, icpt_blk, node_points):
    return (
        slope_blk[:, 0, :, None] * node_points[0]
        + slope_blk[:, 1, :, None] * node_points[1]
        + slope_blk[:, 2, :, None] * node_points[2]
        + icpt_blk[:, :, None]
    )


def apply_update(summed, own_slopes, own_icpt):
    current = jnp.concatenate(
        [own_slopes.astype(jnp.float32), own_icpt.astype(jnp.float32)[None]], axis=0
    )
    return current + summed[:4] / (summed[4:] + 1.0)


def indicators(answers):
    right_b = (answers == 2).astype(jnp.bfloat16)
    answered_b = (answers > 0).astype(jnp.bfloat16)
    wrong_b = (answers == 1).astype(jnp.bfloat16)
    return (right_b, wrong_b, answered_b)


def local(slopes, intercepts, guessing, responses, tile_items, tile_count):
    grid_side = NODES_1D
    tile_size = responses.shape[-1]
    slot_count = responses.shape[1]
    nodes_here = grid_side**3 // lax.axis_size("nodes")
    node_points = node_grid(lax.axis_index("nodes") * nodes_here, nodes_here, grid_side)
    prior_here = log_prior(node_points, grid_side)
    features = jnp.concatenate([node_points, jnp.ones((1, nodes_here), jnp.float32)], axis=0)
    all_slopes, all_icpt, all_guess = (
        lax.all_gather(slopes, "takers", axis=1, tiled=True),
        lax.all_gather(intercepts, "takers", axis=0, tiled=True),
        lax.all_gather(guessing, "takers", axis=0, tiled=True),
    )
    blocks = all_icpt.shape[0] // tile_size
    slope_tab = all_slopes.astype(jnp.float32).reshape(3, blocks, tile_size)
    icpt_tab = all_icpt.astype(jnp.float32).reshape(blocks, tile_size)
    guess_tab = all_guess.astype(jnp.float32).reshape(blocks, tile_size)

    def tables(block_ids, filled):
        live_mask = (jnp.arange(slot_count, dtype=jnp.int32) < filled).astype(jnp.float32)[
            :, None, None
        ]
        slope_blk = jnp.transpose(slope_tab[:, block_ids], (1, 0, 2))
        logits = tile_logits(slope_blk, icpt_tab[block_ids], node_points)
        return (logits, guess_tab[block_ids][:, :, None], live_mask)

    def loglik_block(inputs):
        answers, block_ids, filled = inputs
        logits, guess_rate, live_mask = tables(block_ids, filled)
        correct = guess_rate + (1.0 - guess_rate) * jax.nn.sigmoid(logits)
        log_miss = jnp.log(1.0 - guess_rate) + jax.nn.log_sigmoid(-logits)
        log_right = (jnp.log(correct) * live_mask).astype(jnp.bfloat16)
        log_wrong = (log_miss * live_mask).astype(jnp.bfloat16)
        right_b, wrong_b, answered_b = indicators(answers)
        stacked_ind = jnp.stack([right_b, wrong_b])
        stacked_tab = jnp.stack([log_right, log_wrong])
        matched = lax.dot_general(
            stacked_ind,
            stacked_tab,
            (((0, 1, 3), (0, 1, 2)), ((), ())),
            preferred_element_type=jnp.float32,
        )
        return matched + prior_here

    loglik = lax.map(loglik_block, (responses, tile_items, tile_count)).reshape(-1, nodes_here)
    row_max = jnp.max(loglik, axis=1)
    global_max = lax.pmax(row_max, "nodes")
    weights = jnp.exp(loglik - global_max[:, None])
    moment_here = jnp.einsum("cq,tq->ct", node_points, weights, precision=lax.Precision.HIGHEST)
    row_mass, moment = lax.psum((jnp.sum(weights, axis=1), moment_here), "nodes")
    log_norm = global_max + jnp.log(row_mass)
    posterior_mean = moment / row_mass
    posterior = (
        jnp.exp(loglik - log_norm[:, None]).astype(jnp.bfloat16).reshape(-1, tile_size, nodes_here)
    )

    def stats_block(inputs):
        answers, block_ids, filled, post_blk = inputs
        logits, guess_rate, live_mask = tables(block_ids, filled)
        sig_pos = jax.nn.sigmoid(logits)
        sig_neg = jax.nn.sigmoid(-logits)
        correct = guess_rate + (1.0 - guess_rate) * sig_pos
        right_b, wrong_b, answered_b = indicators(answers)
        stacked_ind = jnp.stack([right_b, answered_b])
        both_mass = lax.dot_general(
            stacked_ind, post_blk, (((2,), (0,)), ((), ())), preferred_element_type=jnp.float32
        )
        correct_mass = both_mass[0]
        node_mass = both_mass[1]
        gradient = (correct_mass - node_mass * correct) * (sig_pos / correct) * live_mask
        fisher = node_mass * (1.0 - guess_rate) * sig_pos * sig_pos * sig_neg / correct * live_mask
        grad_terms = jnp.einsum("kiq,cq->kci", gradient, features, precision=lax.Precision.HIGHEST)
        fisher_terms = jnp.einsum(
            "kiq,cq->kci", fisher, features * features, precision=lax.Precision.HIGHEST
        )
        return jnp.concatenate([grad_terms, fisher_terms], axis=1)

    tile_stats = lax.map(stats_block, (responses, tile_items, tile_count, posterior))
    flat_stats = jnp.transpose(tile_stats, (2, 0, 1, 3)).reshape(8, -1, tile_size)
    item_totals = (
        jnp.zeros((8, blocks, tile_size), jnp.float32).at[:, tile_items.reshape(-1)].add(flat_stats)
    )
    item_totals = item_totals.reshape(8, blocks * tile_size)
    summed = lax.psum_scatter(item_totals, "takers", scatter_dimension=1, tiled=True)
    summed = lax.psum(summed, "nodes")
    new_params = apply_update(summed, slopes, intercepts)
    return (new_params, log_norm, posterior_mean)


def solution(mesh):
    in_specs = (
        P(None, "takers"),
        P("takers"),
        P("takers"),
        P("takers", None, None, None),
        P("takers", None),
        P("takers"),
    )
    out_specs = (P(None, "takers"), P("takers"), P(None, "takers"))
    return jax.shard_map(local, mesh=mesh, in_specs=in_specs, out_specs=out_specs, check_vma=False)
```

profile of v0, /device:TPU:2, one launch (start us, length us, event | category | flops | bytes accessed | tf_op | source)
XLA Modules:
  0.0 1167.5 jit_solution(3456560826222330985)
XLA Ops:
  10.2 105.5 %all_gather.9 = bf16[65536]{0:T(1024)(128)(2,1)S(1)} all-gather(bf16[1024]{0:T(1024)(128)(2,1)} %param.12), channel_id=1, replica_groups=mesh['takers'=64,'nodes'=8] {'takers'}, dimensions={0}, use_global_device_ids=true | all-gather | bytes 133120 | tf_op jit(solution)/shard_map/all_gather | solution.py:61
  115.7 97.4 %all_gather.11 = bf16[65536]{0:T(1024)(128)(2,1)S(1)} all-gather(bf16[1024]{0:T(1024)(128)(2,1)} %param.11), channel_id=1, replica_groups=mesh['takers'=64,'nodes'=8] {'takers'}, dimensions={0}, use_global_device_ids=true | all-gather | bytes 133120 | tf_op jit(solution)/shard_map/all_gather | solution.py:60
  213.1 98.1 %all_gather.10 = bf16[3,65536]{1,0:T(4,128)(2,1)S(1)} all-gather(bf16[3,1024]{1,0:T(4,128)(2,1)} %param.10), channel_id=1, replica_groups=mesh['takers'=64,'nodes'=8] {'takers'}, dimensions={1}, use_global_device_ids=true | all-gather | bytes 399360 | tf_op jit(solution)/shard_map/all_gather | solution.py:59
  311.5 36.9 %while.21 = (s32[]{:T(128)}, f32[4,128,512]{2,1,0:T(8,128)S(1)}, s32[4,12,128,128]{3,2,1,0:T(8,128)}, s32[4,12]{1,0:T(4,128)S(1)}, f32[512,128]{1,0:T(8,128)S(1)...) while((s32[]{:T(128)}, f32[4,128,512]{2,1,0:T(8,128)S(1)}, ...), condition=%wide.region_4.5_spmd, body=%wide.region_3.4_spmd.sunk | while | flops 423168576 | bytes 8348177 | solution.py:94
  315.9 4.2 multiply_convert_fusion.2
  325.1 4.2 multiply_convert_fusion.2
  334.4 4.2 multiply_convert_fusion.2
  343.6 4.2 multiply_convert_fusion.2
  348.6 12.4 %pmax.7 = f32[512]{0:T(512)S(1)} all-reduce(f32[512]{0:T(512)S(1)} %bitcast.192), channel_id=1, replica_groups=mesh['takers'=64,'nodes'=8] {'nodes'}, use_global_device_ids=true, to_apply=%region_6.7 | all-reduce | flops 512 | bytes 4096 | tf_op jit(solution)/shard_map/pmax | solution.py:96
  361.3 12.7 %psum.21 = f32[512]{0:T(512)S(1)} all-reduce(f32[512]{0:T(512)S(1)} %bitcast.193), channel_id=1, replica_groups=mesh['takers'=64,'nodes'=8] {'nodes'}, use_global_device_ids=true, to_apply=%region_8.9 | all-reduce | flops 512 | bytes 4096 | tf_op jit(solution)/shard_map/psum | solution.py:99
  375.0 69.3 %while.22 = (s32[]{:T(128)}, f32[4,12,8,128]{3,2,1,0:T(8,128)S(1)}, s32[4,12,128,128]{3,2,1,0:T(8,128)}, bf16[4,128,512]{2,1,0:T(8,128)(2,1)}, s32[4,12]{1,0:T(4...) while((s32[]{:T(128)}, f32[4,12,8,128]{3,2,1,0:T(8,128)S(1)}, ...), condition=%wide.region_10.11_spmd, body=%wide.region_9.10_spmd.sunk | while | flops 507263552 | bytes 27296860 | solution.py:127
  379.9 1.9 fusion.147
  381.8 5.1 fusion.152
  386.8 5.4 fusion.151
  397.2 1.9 fusion.147
  399.1 5.1 fusion.152
  404.2 5.4 fusion.151
  416.4 5.1 fusion.152
  421.5 5.4 fusion.151
  433.7 5.1 fusion.152
  438.8 5.4 fusion.151
  444.5 2.2 scatter_fusion
  449.3 685.7 %reduce-scatter.2.cloned.1.call-done = f32[8,1024]{1,0:T(8,128)} async-done(((f32[8,65536]{1,0:T(8,128)}), f32[8,1024]{1,0:T(8,128)}) %reduce-scatter.2.cloned.1.call-update) | async-done | bytes 32784 | tf_op jit(solution)/shard_map/reduce_scatter | solution.py:133
  1135.0 24.5 %all-reduce.1 = (f32[8,1024]{1,0:T(8,128)S(1)}, f32[3,512]{1,0:T(4,128)S(1)}) all-reduce(f32[8,1024]{1,0:T(8,128)} %reduce-scatter.2.cloned.1.call-done, f32[3,512]{1,0:T(4,128)S(1)} %fusion.109), channel_id=1, replica_groups=mesh['takers'=64,'nodes'=8] {'nodes'}, use_global_device_ids=true, to_apply=%region_13.14 | all-reduce | flops 9728 | bytes 77824 | tf_op jit(solution)/shard_map/psum | solution.py:134
  (192 shorter events, 50.6 us)
Async XLA Ops:
  7.2 304.3 %copy-start.12 = (s32[4,12]{1,0:T(4,128)S(1)}, s32[4,12]{1,0:T(4,128)}, u32[]{:S(2)}) copy-start(s32[4,12]{1,0:T(4,128)} %param.14) | copy-start | bytes 580
  7.2 304.3 %copy-start.14 = (s32[4]{0:T(128)S(1)}, s32[4]{0:T(128)}, u32[]{:S(2)}) copy-start(s32[4]{0:T(128)} %param.15) | copy-start | bytes 52
  7.2 1127.8 %reduce-scatter.2.cloned.1.call-start = ((), (), s32[]{:S(2)}) async-start(), calls=%async_computation.1 | async-start | bytes 2129920 | tf_op jit(solution)/shard_map/reduce_scatter | solution.py:133
  7.3 304.2 %copy-start.4 = (s32[1,512]{1,0:T(1,128)}, s32[1,512]{1,0:T(1,128)S(1)}, u32[]{:S(2)}) copy-start(s32[1,512]{1,0:T(1,128)S(1)} %and_select_fusion.7) | copy-start | bytes 6148
  7.3 1.4 copy-start.8
  7.3 304.1 %copy-start.6 = (s32[1,512]{1,0:T(1,128)}, s32[1,512]{1,0:T(1,128)S(1)}, u32[]{:S(2)}) copy-start(s32[1,512]{1,0:T(1,128)S(1)} %get-tuple-element.285) | copy-start | bytes 6148
  374.0 1.0 copy-start.11
  375.0 69.5 %copy-start.13 = (s32[48]{0:T(128)S(1)}, s32[48]{0:T(128)}, u32[]{:S(2)}) copy-start(s32[48]{0:T(128)} %fusion.108) | copy-start | bytes 580
  375.0 3.2 copy-start.1
  386.8 5.5 copy-start.2
  392.3 3.2 copy-start.1
  404.2 5.5 copy-start.2
  409.7 3.2 copy-start.1
  421.5 5.5 copy-start.2
  427.0 3.2 copy-start.1
  438.8 5.5 copy-start.2
  444.3 3.8 copy-start.10
  444.3 4.0 copy-start.5
  444.3 4.0 copy-start.7
  444.4 4.0 copy-start.9
  444.5 715.5 %copy-start.3 = (bf16[3,1024]{1,0:T(4,128)(2,1)S(1)}, bf16[3,1024]{1,0:T(4,128)(2,1)}, u32[]{:S(2)}) copy-start(bf16[3,1024]{1,0:T(4,128)(2,1)} %param.10) | copy-start | bytes 18436
  446.7 1.3 copy-start
Sparse Core Ops, SparseCore 0:
  448.2 686.7 reduce-scatter.1
where the time goes:
time: 1170 us
  waiting for transfers between devices  686 us (59%)
  blocking collectives  351 us (30%)
  matrix products  52.9 us (5%)
  other arithmetic  35.2 us (3%)
  local copies, waits for them, and re-layouts  27.2 us (2%)
  between operations  15 us (1%)
    reduce_scatter x1, waiting for transfers between devices, local(): lax.psum_scatter(item_totals, 'takers', scatter_dimension=1, tiled=True)  686 us
    all_gather x1, blocking collectives, local(): lax.all_gather(guessing, 'takers', axis=0, tiled=True)  106 us
    all_gather x1, blocking collectives, local(): lax.all_gather(slopes, 'takers', axis=1, tiled=True)  98.1 us
    all_gather x1, blocking collectives, local(): lax.all_gather(intercepts, 'takers', axis=0, tiled=True)  97.4 us
    psum x1, blocking collectives, local(): summed = lax.psum(summed, 'nodes')  24.5 us
  transfers between devices with their start and end apart: 1, of which 1 were waited for; matrix products, arithmetic and copies ran while one was open for 0% of the time, Pallas kernels for 0%

commit v1 on v0

--- a/solution.py
+++ b/solution.py
@@ -58,7 +58,9 @@
     all_slopes, all_icpt, all_guess = (
         lax.all_gather(slopes, "takers", axis=1, tiled=True),
         lax.all_gather(intercepts, "takers", axis=0, tiled=True),
-        lax.all_gather(guessing, "takers", axis=0, tiled=True),
+        jnp.concatenate(
+            lax.all_to_all(jnp.stack([guessing] * lax.axis_size("takers")), "takers", 0, 0), axis=0
+        ),
     )
     blocks = all_icpt.shape[0] // tile_size
     slope_tab = all_slopes.astype(jnp.float32).reshape(3, blocks, tile_size)

time: 1170 us -> 1090 us (0.932)
  blocking collectives: 351 us -> 247 us
  starting transfers between devices: 0.04 us -> 18.7 us
    all_gather x1 -> x0, blocking collectives: 106 us -> none  [local(): lax.all_gather(guessing, 'takers', axis=0, tiled=True)]
    all_to_all x0 -> x1, starting transfers between devices: none -> 18.6 us  [local(): lax.all_to_all(jnp.stack([guessing] * lax.axis_size('takers')), 'takers',...]
  transfers between devices with their start and end apart: 1 -> 2, of which waited for: 1 -> 1; matrix products, arithmetic and copies ran while one was open for 0% -> 0% of each run, Pallas kernels for 0% -> 0%
where the time goes in v1:
time: 1090 us
  waiting for transfers between devices  688 us (63%)
  blocking collectives  247 us (23%)
  matrix products  52.9 us (5%)
  other arithmetic  36.9 us (3%)
  local copies, waits for them, and re-layouts  29.7 us (3%)
  starting transfers between devices  18.7 us (2%)
  between operations  15 us (1%)
    reduce_scatter x1, waiting for transfers between devices, local(): lax.psum_scatter(item_totals, 'takers', scatter_dimension=1, tiled=True)  688 us
    all_gather x1, blocking collectives, local(): lax.all_gather(slopes, 'takers', axis=1, tiled=True)  99.8 us
    all_gather x1, blocking collectives, local(): lax.all_gather(intercepts, 'takers', axis=0, tiled=True)  97.5 us
    psum x1, blocking collectives, local(): summed = lax.psum(summed, 'nodes')  24.5 us
  transfers between devices with their start and end apart: 2, of which 1 were waited for; matrix products, arithmetic and copies ran while one was open for 0% of the time, Pallas kernels for 0%

profile of v1, /device:TPU:2, one launch (start us, length us, event | category | flops | bytes accessed | tf_op | source)
XLA Modules:
  0.0 1089.1 jit_solution(72841714430214098)
XLA Ops:
  10.6 18.6 %all-to-all-start = ((bf16[64,2,512]{2,1,0:T(2,128)(2,1)}), bf16[64,2,512]{2,1,0:T(2,128)(2,1)S(1)}, u32[]{:S(2)}, u32[]{:S(2)}) async-start(bf16[64,2,512]{2,1,0:T(2,128)(2,1)} %reshape.582), calls=%async_computation | async-start | bytes 262144 | tf_op jit(solution)/shard_map/all_to_all | solution.py:62
  32.4 99.8 %all_gather.6 = bf16[3,65536]{1,0:T(4,128)(2,1)S(1)} all-gather(bf16[3,1024]{1,0:T(4,128)(2,1)} %param.10), channel_id=1, replica_groups=mesh['takers'=64,'nodes'=8] {'takers'}, dimensions={1}, use_global_device_ids=true | all-gather | bytes 399360 | tf_op jit(solution)/shard_map/all_gather | solution.py:59
  132.2 97.5 %all_gather.7 = bf16[65536]{0:T(1024)(128)(2,1)S(1)} all-gather(bf16[1024]{0:T(1024)(128)(2,1)} %param.11), channel_id=1, replica_groups=mesh['takers'=64,'nodes'=8] {'takers'}, dimensions={0}, use_global_device_ids=true | all-gather | bytes 133120 | tf_op jit(solution)/shard_map/all_gather | solution.py:60
  230.2 37.1 %while.21 = (s32[]{:T(128)}, f32[4,128,512]{2,1,0:T(8,128)S(1)}, s32[4,12,128,128]{3,2,1,0:T(8,128)}, s32[4,12]{1,0:T(4,128)S(1)}, f32[512,128]{1,0:T(8,128)S(1)...) while((s32[]{:T(128)}, f32[4,128,512]{2,1,0:T(8,128)S(1)}, ...), condition=%wide.region_4.5_spmd, body=%wide.region_3.4_spmd.sunk | while | flops 423168576 | bytes 8348177 | solution.py:96
  234.7 4.2 multiply_convert_fusion.2
  244.0 4.2 multiply_convert_fusion.2
  253.3 4.2 multiply_convert_fusion.2
  262.5 4.2 multiply_convert_fusion.2
  267.5 12.4 %pmax.7 = f32[512]{0:T(512)S(1)} all-reduce(f32[512]{0:T(512)S(1)} %bitcast.191), channel_id=1, replica_groups=mesh['takers'=64,'nodes'=8] {'nodes'}, use_global_device_ids=true, to_apply=%region_6.7 | all-reduce | flops 512 | bytes 4096 | tf_op jit(solution)/shard_map/pmax | solution.py:98
  280.2 12.7 %psum.21 = f32[512]{0:T(512)S(1)} all-reduce(f32[512]{0:T(512)S(1)} %bitcast.192), channel_id=1, replica_groups=mesh['takers'=64,'nodes'=8] {'nodes'}, use_global_device_ids=true, to_apply=%region_8.9 | all-reduce | flops 512 | bytes 4096 | tf_op jit(solution)/shard_map/psum | solution.py:101
  293.9 69.5 %while.22 = (s32[]{:T(128)}, f32[4,12,8,128]{3,2,1,0:T(8,128)S(1)}, s32[4,12,128,128]{3,2,1,0:T(8,128)}, bf16[4,128,512]{2,1,0:T(8,128)(2,1)}, s32[4,12]{1,0:T(4...) while((s32[]{:T(128)}, f32[4,12,8,128]{3,2,1,0:T(8,128)S(1)}, ...), condition=%wide.region_10.11_spmd, body=%wide.region_9.10_spmd.sunk | while | flops 507263552 | bytes 27296860 | solution.py:129
  298.8 1.9 fusion.147
  300.7 5.1 fusion.152
  305.8 5.4 fusion.151
  316.2 1.9 fusion.147
  318.1 5.1 fusion.152
  323.2 5.4 fusion.151
  335.5 5.1 fusion.152
  340.5 5.4 fusion.151
  352.8 5.1 fusion.152
  357.9 5.4 fusion.151
  363.6 2.2 scatter_fusion
  368.4 688.2 %reduce-scatter.2.cloned.1.call-done = f32[8,1024]{1,0:T(8,128)} async-done(((f32[8,65536]{1,0:T(8,128)}), f32[8,1024]{1,0:T(8,128)}) %reduce-scatter.2.cloned.1.call-update) | async-done | bytes 32784 | tf_op jit(solution)/shard_map/reduce_scatter | solution.py:135
  1056.6 24.5 %all-reduce.1 = (f32[8,1024]{1,0:T(8,128)S(1)}, f32[3,512]{1,0:T(4,128)S(1)}) all-reduce(f32[8,1024]{1,0:T(8,128)} %reduce-scatter.2.cloned.1.call-done, f32[3,512]{1,0:T(4,128)S(1)} %fusion.109), channel_id=1, replica_groups=mesh['takers'=64,'nodes'=8] {'nodes'}, use_global_device_ids=true, to_apply=%region_13.14 | all-reduce | flops 9728 | bytes 77824 | tf_op jit(solution)/shard_map/psum | solution.py:136
  (198 shorter events, 54.8 us)
Async XLA Ops:
  7.2 223.0 %copy-start.12 = (s32[4,12]{1,0:T(4,128)S(1)}, s32[4,12]{1,0:T(4,128)}, u32[]{:S(2)}) copy-start(s32[4,12]{1,0:T(4,128)} %param.14) | copy-start | bytes 580
  7.2 223.0 %copy-start.14 = (s32[4]{0:T(128)S(1)}, s32[4]{0:T(128)}, u32[]{:S(2)}) copy-start(s32[4]{0:T(128)} %param.15) | copy-start | bytes 52
  10.6 219.2 %all-to-all-start = ((bf16[64,2,512]{2,1,0:T(2,128)(2,1)}), bf16[64,2,512]{2,1,0:T(2,128)(2,1)S(1)}, u32[]{:S(2)}, u32[]{:S(2)}) async-start(bf16[64,2,512]{2,1,0:T(2,128)(2,1)} %reshape.582), calls=%async_computation | async-start | bytes 262144 | tf_op jit(solution)/shard_map/all_to_all | solution.py:62
  29.3 1027.3 %reduce-scatter.2.cloned.1.call-start = ((), (), s32[]{:S(2)}) async-start(), calls=%async_computation.2 | async-start | bytes 2129920 | tf_op jit(solution)/shard_map/reduce_scatter | solution.py:135
  29.4 200.8 %copy-start.4 = (s32[1,512]{1,0:T(1,128)}, s32[1,512]{1,0:T(1,128)S(1)}, u32[]{:S(2)}) copy-start(s32[1,512]{1,0:T(1,128)S(1)} %and_select_fusion.7) | copy-start | bytes 6148
  29.4 1.5 copy-start.8
  29.4 200.8 %copy-start.6 = (s32[1,512]{1,0:T(1,128)}, s32[1,512]{1,0:T(1,128)S(1)}, u32[]{:S(2)}) copy-start(s32[1,512]{1,0:T(1,128)S(1)} %get-tuple-element.285) | copy-start | bytes 6148
  292.9 1.0 copy-start.11
  293.9 69.7 %copy-start.13 = (s32[48]{0:T(128)S(1)}, s32[48]{0:T(128)}, u32[]{:S(2)}) copy-start(s32[48]{0:T(128)} %fusion.108) | copy-start | bytes 580
  293.9 3.2 copy-start.1
  305.8 5.5 copy-start.2
  311.3 3.2 copy-start.1
  323.2 5.5 copy-start.2
  328.7 3.2 copy-start.1
  340.5 5.5 copy-start.2
  346.0 3.2 copy-start.1
  357.9 5.5 copy-start.2
  363.4 3.8 copy-start.10
  363.4 4.0 copy-start.5
  363.4 4.0 copy-start.7
  363.4 4.0 copy-start.9
  363.6 718.0 %copy-start.3 = (bf16[3,1024]{1,0:T(4,128)(2,1)S(1)}, bf16[3,1024]{1,0:T(4,128)(2,1)}, u32[]{:S(2)}) copy-start(bf16[3,1024]{1,0:T(4,128)(2,1)} %param.10) | copy-start | bytes 18436
  365.8 1.3 copy-start
Sparse Core Ops, SparseCore 0:
  367.3 689.2 reduce-scatter.1
